TPU v7x, 32 devices: a whole 2x2x4 slice. The times are simulated.
32 devices in a mesh: groups: 1, dp: 32 (over z, y, x, core).
Axes of the slice: x: 2, y: 2, z: 4, core: 2. Of those that a mesh axis runs over, the one named last changes fastest.
Arguments:
- activations: bfloat16 [128, 8192], P(('groups', 'dp')), may hold values from -6 to 6
- cotangent: bfloat16 [128, 8192], P(('groups', 'dp')), may hold values from -6 to 6
- w_gate: bfloat16 [28672, 8192], P('dp'), may hold values from -0.0625 to 0.0625
- w_up: bfloat16 [28672, 8192], P('dp'), may hold values from -0.0625 to 0.0625
- w_down: bfloat16 [28672, 8192], P('dp'), may hold values from -0.03125 to 0.03125
- proj_model: bfloat16 [8192, 192], P('dp'), may hold values from -0.0625 to 0.0625
- proj_hidden: bfloat16 [28672, 192], P('dp'), may hold values from -0.03125 to 0.03125
- seq_ids: int32 [128], P('groups'), may hold values from 0 to 15, never falling along the last dimension, each value on 1 to 16 neighbouring positions
- targets: bfloat16 [256, 3, 64, 64], P(('groups', 'dp')), may hold values from -24 to 24
- target_domain: int32 [256], P(('groups', 'dp')), may hold values from 0 to 31, never falling along the last dimension, each value on 1 to 16 neighbouring positions
Outputs:
- sketches: float32 [16, 3, 64, 64], P('groups')
- scores: float32 [16, 32], P('groups')
Inputs may be any that keep to these rules, and one draw needn't show every extreme that they name: `seq_ids`: never falling along the tokens; each of the 16 sequences has 1 to 16 tokens, one exactly 16. `target_domain`: never falling along the target examples; each of the 32 domains has 1 to 16 examples, one exactly 16.
All inputs are finite; a program needn't handle non-finite values.
Results may differ from a plain program's by a relative error of at most 0.0032.
Values may be sent and summed in bfloat16 or wider, within the bound.
A program may use at most 128 MiB of HBM per device.

v0:
```python
import functools

import jax
import jax.numpy as jnp
from jax import lax
from jax.experimental import pallas as pl
from jax.experimental.pallas import tpu as pltpu
from jax.sharding import PartitionSpec as P

DOMAINS = 32
SEQS = 16
MESH = pl.DeviceIdType.MESH
ROUTES = 2
CHUNKS = 8


def routes_of(n):
    core = (2, 1)
    if n == 32:
        z, y, x = (4, 8), (2, 4), (2, 2)
        return ((z, y, x, core), (z, x, y, core))
    if n == 128:
        y, x = (8, 16), (8, 2)
        return ((y, x, core), (x, y, core))
    rest = (n // 2, 2)
    return ((rest, core), (rest, core))


def moved(index, size, stride, by):
    coord = lax.rem(lax.div(index, stride), size)
    return index + (lax.rem(coord + by, size) - coord) * stride


def kernel(
    n,
    act_ref, cot_ref, wg_ref, wu_ref, wd_ref, pm_ref, ph_ref, seq_ref, tgt_ref, dom_ref,
    sk_ref, score_ref,
    wbuf, xg, xs, gacc, uacc, dacc, part, rsbuf, red, vg, lm, tf, prod, msg, msgbuf,
    w_sem, own_sem, ag_send, ag_recv, rs_send, rs_recv, bc_send, bc_recv, sc_send, sc_recv,
):
    me = lax.axis_index("dp")
    half = n // 2
    routes = routes_of(n)
    tokens, width = xs.shape[2], xs.shape[3]
    per_route = CHUNKS // ROUTES
    rank = pm_ref.shape[1] // 3
    hidden_units = wg_ref.shape[0]
    own_rows = act_ref.shape[1]

    def weight_copy(m, c):
        source = (wg_ref, wu_ref, wd_ref)[m]
        return pltpu.make_async_copy(
            source.at[:, pl.ds(c * width, width)], wbuf.at[m, c], w_sem.at[m, c]
        )

    own_copies = []
    for a, source in enumerate((act_ref, cot_ref)):
        for r in range(ROUTES):
            copy = pltpu.make_async_copy(source.at[r], xg.at[a, r, me], own_sem.at[a, r])
            copy.start()
            own_copies.append(copy)

    barrier = pltpu.get_barrier_semaphore()

    def greet(d, carry):
        pl.semaphore_signal(
            barrier, inc=1, device_id={"dp": lax.rem(me + d, n)}, device_id_type=MESH
        )
        return carry

    lax.fori_loop(1, n, greet, 0)
    for c in range(CHUNKS):
        weight_copy(0, c).start()
        weight_copy(1, c).start()
    for c in range(CHUNKS):
        weight_copy(2, c).start()
    for copy in own_copies:
        copy.wait()
    pl.semaphore_wait(barrier, n - 1)

    def held_before(r, stage):
        count = 1
        for size, _ in routes[r][:stage]:
            count = count * size
        return count

    def send_stage(a, r, stage):
        size, stride = routes[r][stage]
        done = routes[r][:stage]

        def step(i, carry):
            t, d = lax.div(i, size - 1), lax.rem(i, size - 1) + 1
            block = me
            for done_size, done_stride in done:
                block = moved(block, done_size, done_stride, done_size - lax.rem(t, done_size))
                t = lax.div(t, done_size)
            pltpu.make_async_remote_copy(
                src_ref=xg.at[a, r, block],
                dst_ref=xg.at[a, r, block],
                send_sem=ag_send.at[a, r],
                recv_sem=ag_recv.at[a, r, stage],
                device_id={"dp": moved(me, size, stride, d)},
                device_id_type=MESH,
            ).start()
            return carry

        lax.fori_loop(0, held_before(r, stage) * (size - 1), step, 0)

    def take_stage(a, r, stage):
        count = held_before(r, stage) * (routes[r][stage][0] - 1)
        blocks = xg.at[a, r, pl.ds(0, count)]
        pltpu.make_async_copy(blocks, blocks, ag_recv.at[a, r, stage]).wait()

    stages = len(routes[0])
    for a in range(2):
        for r in range(ROUTES):
            send_stage(a, r, 0)
    examples = tgt_ref.shape[0]
    for e in range(examples):
        tf[e] = tgt_ref[e].astype(jnp.float32)
    for stage in range(1, stages):
        for r in range(ROUTES):
            take_stage(0, r, stage - 1)
            send_stage(0, r, stage)

    def lay_out(a, r, q):
        c = r * per_route + q
        group = 16 // own_rows

        def step(g, carry):
            pieces = [
                xg[a, r, g * group + i, :, pl.ds(pl.multiple_of(q * width, width), width)].astype(jnp.float32)
                for i in range(group)
            ]
            xs[a, c, pl.ds(pl.multiple_of(g * 16, 16), 16), :] = jnp.concatenate(pieces, 0).astype(
                jnp.bfloat16
            )
            return carry

        lax.fori_loop(0, tokens // 16, step, 0, unroll=True)

    contract = (((1,), (1,)), ((), ()))

    def add_product(acc, a, m, c):
        acc[...] += lax.dot_general(
            xs[a, c], wbuf[m, c], contract, preferred_element_type=jnp.float32
        )

    gacc[...] = jnp.zeros_like(gacc)
    uacc[...] = jnp.zeros_like(uacc)
    dacc[...] = jnp.zeros_like(dacc)
    def relay(stage):
        if stage < stages:
            for r in range(ROUTES):
                take_stage(1, r, stage - 1)
                send_stage(1, r, stage)

    for r in range(ROUTES):
        take_stage(0, r, stages - 1)

        def gate_up(q, carry, r=r):
            c = r * per_route + q
            lay_out(0, r, q)
            weight_copy(0, c).wait()
            add_product(gacc, 0, 0, c)
            weight_copy(1, c).wait()
            add_product(uacc, 0, 1, c)
            return carry

        for part_of in range(2):
            relay(2 * r + part_of + 1)
            first = part_of * per_route // 2
            lax.fori_loop(first, first + per_route // 2, gate_up, 0)

    for r in range(ROUTES):
        take_stage(1, r, stages - 1)

        def down(q, carry, r=r):
            c = r * per_route + q
            lay_out(1, r, q)
            weight_copy(2, c).wait()
            add_product(dacc, 1, 2, c)
            return carry

        lax.fori_loop(0, per_route, down, 0)

    in_down = out_gate = out_up = jnp.zeros((tokens, rank), jnp.float32)
    for off in range(0, hidden_units, 256):
        cols = slice(off, min(off + 256, hidden_units))
        gate, up, grad = gacc[:, cols], uacc[:, cols], dacc[:, cols]
        sig = jax.nn.sigmoid(gate)
        silu = gate * sig
        hidden = (silu * up).astype(jnp.bfloat16)
        grad_gate = (grad * up * sig * (1.0 + gate * (1.0 - sig))).astype(jnp.bfloat16)
        grad_up = (grad * silu).astype(jnp.bfloat16)
        ph = ph_ref[cols, :]
        in_down += jnp.dot(hidden, ph[:, :rank], preferred_element_type=jnp.float32)
        out_gate += jnp.dot(grad_gate, ph[:, rank : 2 * rank], preferred_element_type=jnp.float32)
        out_up += jnp.dot(grad_up, ph[:, 2 * rank :], preferred_element_type=jnp.float32)

    window = pm_ref.shape[0]
    model_cols = CHUNKS * width // n
    start = lax.div(me * model_cols, window) * window
    own_chunk = lax.div(start, width)
    own_cols = pl.ds(pl.multiple_of(lax.rem(start, width), window), window)
    pm = pm_ref[...]
    rights = jnp.dot(xs[0, own_chunk, :, own_cols], pm[:, : 2 * rank], preferred_element_type=jnp.float32)
    out_down = jnp.dot(xs[1, own_chunk, :, own_cols], pm[:, 2 * rank :], preferred_element_type=jnp.float32)
    part[:, : 2 * rank] = jnp.concatenate([out_gate, out_up], 1)
    part[:, 2 * rank : 4 * rank] = jnp.concatenate([in_down, out_down], 1)
    part[:, 4 * rank :] = rights

    odd = lax.rem(me, 2)
    mine = lax.div(me, 2)

    def rows(j):
        return pl.ds(pl.multiple_of(j * 8, 8), 8)

    def to_reducer(d):
        j = lax.rem(mine + d, half)
        return pltpu.make_async_remote_copy(
            src_ref=part.at[rows(j)],
            dst_ref=rsbuf.at[me],
            send_sem=rs_send,
            recv_sem=rs_recv,
            device_id={"dp": 2 * j},
            device_id_type=MESH,
        )

    def scatter(d, carry):
        to_reducer(d).start()
        return carry

    lax.fori_loop(1, half, scatter, 0)

    @pl.when(odd == 1)
    def _():
        to_reducer(0).start()
        pltpu.make_async_copy(part, part, rs_send).wait()

    @pl.when(odd == 0)
    def _():
        pltpu.make_async_copy(part.at[rows(mine)], rsbuf.at[me], rs_recv).start()
        sent = part.at[pl.ds(0, 8 * (half - 1))]
        pltpu.make_async_copy(sent, sent, rs_send).wait()
        pltpu.make_async_copy(rsbuf, rsbuf, rs_recv).wait()
        red[...] = jnp.sum(rsbuf[...], 0)
        pltpu.make_async_copy(red, vg.at[rows(mine)], bc_recv).start()

        def share(d, carry):
            pltpu.make_async_remote_copy(
                src_ref=red,
                dst_ref=vg.at[rows(mine)],
                send_sem=bc_send,
                recv_sem=bc_recv,
                device_id={"dp": lax.rem(me + d, n)},
                device_id_type=MESH,
            ).start()
            return carry

        lax.fori_loop(1, n, share, 0)
        sent = rsbuf.at[pl.ds(0, n - 1)]
        pltpu.make_async_copy(sent, sent, bc_send).wait()

    for a in range(2):
        for r in range(ROUTES):
            count = 0
            for stage in range(stages):
                count += held_before(r, stage) * (routes[r][stage][0] - 1)
            sent = xg.at[a, r, pl.ds(0, count)]
            pltpu.make_async_copy(sent, sent, ag_send.at[a, r]).wait()

    pltpu.make_async_copy(vg, vg, bc_recv).wait()

    seq = seq_ref[...]
    outs = vg[:, : 2 * rank].T
    mixed = vg[:, 2 * rank : 4 * rank]
    ins = vg[:, 4 * rank :]
    lefts = (outs[:rank], outs[rank:], mixed.T[:rank])
    rights = (ins[:, :rank], ins[:, rank:], mixed[:, rank:])
    for k in range(3):
        left, right = lefts[k], rights[k]
        left_hi = left.astype(jnp.bfloat16).astype(jnp.float32)
        left_lo = left - left_hi
        for s in range(SEQS):
            here = seq == s
            hi = jnp.where(here, left_hi, 0.0).astype(jnp.bfloat16)
            lo = jnp.where(here, left_lo, 0.0).astype(jnp.bfloat16)
            block = slice(s * rank, (s + 1) * rank)
            lm[block, :tokens] = hi
            lm[block, tokens : 2 * tokens] = lo
            lm[block, 2 * tokens :] = hi
        right_hi = right.astype(jnp.bfloat16)
        right_lo = (right - right_hi.astype(jnp.float32)).astype(jnp.bfloat16)
        sketch = jnp.dot(
            lm[...], jnp.concatenate([right_hi, right_hi, right_lo], 0), preferred_element_type=jnp.float32
        )
        sk_ref[:, k] = sketch.reshape(SEQS, rank, rank)

    def score(s, carry):
        squares = jnp.zeros((8, rank), jnp.float32)
        sums = [squares] * examples
        for k in range(3):
            block = sk_ref[s, k]
            for i in range(0, rank, 8):
                piece = block[i : i + 8]
                squares = squares + piece * piece
                for e in range(examples):
                    sums[e] = sums[e] + piece * tf[e, k, i : i + 8, :]
        for e in range(examples):
            prod[e, s] = sums[e]
        prod[examples, s] = squares
        return carry

    lax.fori_loop(0, SEQS, score, 0)

    def column_of(e):
        return jnp.sum(jnp.sum(prod[e], 1), 1, keepdims=True)

    top = SEQS // 2
    lane = lax.broadcasted_iota(jnp.int32, (top, 128), 1)
    folded = jnp.zeros((top, 128), jnp.float32)
    for e in range(examples):
        column = column_of(e)
        domain = dom_ref[e]
        folded += jnp.where(lane == domain, column[:top], 0.0)
        folded += jnp.where(lane == domain + DOMAINS, column[top:], 0.0)
        folded += jnp.where(lane == domain + 2 * DOMAINS, 1.0, 0.0)
    inverse_norm = lax.rsqrt(column_of(examples) + 1e-06)
    msg[...] = folded
    pltpu.make_async_copy(msg, msgbuf.at[me], sc_recv).start()

    def spread(d, carry):
        pltpu.make_async_remote_copy(
            src_ref=msg,
            dst_ref=msgbuf.at[me],
            send_sem=sc_send,
            recv_sem=sc_recv,
            device_id={"dp": lax.rem(me + d, n)},
            device_id_type=MESH,
        ).start()
        return carry

    lax.fori_loop(1, n, spread, 0)
    sent = msgbuf.at[pl.ds(0, n - 1)]
    pltpu.make_async_copy(sent, sent, sc_send).wait()
    pltpu.make_async_copy(msgbuf, msgbuf, sc_recv).wait()
    total = jnp.sum(msgbuf[...], 0)
    counts = total[:, 2 * DOMAINS : 3 * DOMAINS]
    score_ref[:top] = total[:, :DOMAINS] / counts * inverse_norm[:top]
    score_ref[top:] = total[:, DOMAINS : 2 * DOMAINS] / counts * inverse_norm[top:]


def on_device(n, activations, cotangent, w_gate, w_up, w_down, proj_model, proj_hidden, seq_ids, targets, target_domain):
    own_rows, model = activations.shape
    tokens = n * own_rows
    hidden_units = w_gate.shape[0]
    model_cols, features = proj_model.shape
    rank = features // 3
    width = model // CHUNKS
    stages = len(routes_of(n)[0])

    def by_route(x):
        return x.reshape(own_rows, ROUTES, model // ROUTES).transpose(1, 0, 2)

    if model_cols < 128:
        me = lax.axis_index("dp")
        padded = jnp.zeros((128, features), proj_model.dtype)
        proj_model = lax.dynamic_update_slice(padded, proj_model, ((me * model_cols) % 128, 0))
    vmem = pl.BlockSpec(memory_space=pltpu.VMEM)
    hbm = pl.BlockSpec(memory_space=pl.ANY)
    smem = pl.BlockSpec(memory_space=pltpu.SMEM)
    f32, bf16 = jnp.float32, jnp.bfloat16
    dma = pltpu.SemaphoreType.DMA
    return pl.pallas_call(
        functools.partial(kernel, n),
        out_shape=(
            jax.ShapeDtypeStruct((SEQS, 3, rank, rank), f32),
            jax.ShapeDtypeStruct((SEQS, DOMAINS), f32),
        ),
        in_specs=[vmem, vmem, hbm, hbm, hbm, vmem, vmem, vmem, vmem, smem],
        out_specs=(vmem, vmem),
        scratch_shapes=[
            pltpu.VMEM((3, CHUNKS, hidden_units, width), bf16),
            pltpu.VMEM((2, ROUTES, n, own_rows, model // ROUTES), bf16),
            pltpu.VMEM((2, CHUNKS, tokens, width), bf16),
            pltpu.VMEM((tokens, hidden_units), f32),
            pltpu.VMEM((tokens, hidden_units), f32),
            pltpu.VMEM((tokens, hidden_units), f32),
            pltpu.VMEM((tokens, 2 * features), f32),
            pltpu.VMEM((n, 8, 2 * features), f32),
            pltpu.VMEM((8, 2 * features), f32),
            pltpu.VMEM((tokens, 2 * features), f32),
            pltpu.VMEM((SEQS * rank, 3 * tokens), bf16),
            pltpu.VMEM(targets.shape, f32),
            pltpu.VMEM((targets.shape[0] + 1, SEQS, 8, rank), f32),
            pltpu.VMEM((SEQS // 2, 128), f32),
            pltpu.VMEM((n, SEQS // 2, 128), f32),
            dma((3, CHUNKS)),
            dma((2, ROUTES)),
            dma((2, ROUTES)),
            dma((2, ROUTES, stages)),
            dma(()),
            dma(()),
            dma(()),
            dma(()),
            dma(()),
            dma(()),
        ],
        compiler_params=pltpu.CompilerParams(
            collective_id=0, has_side_effects=True, vmem_limit_bytes=67000000
        ),
        name="sketch_scores",
    )(
        by_route(activations), by_route(cotangent), w_gate, w_up, w_down, proj_model, proj_hidden,
        seq_ids.reshape(1, tokens), targets, target_domain,
    )


def solution(mesh):
    in_specs = (
        P(("groups", "dp"), None),
        P(("groups", "dp"), None),
        P("dp", None),
        P("dp", None),
        P("dp", None),
        P("dp", None),
        P("dp", None),
        P("groups"),
        P(("groups", "dp"), None, None, None),
        P(("groups", "dp")),
    )
    out_specs = (P("groups", None, None, None), P("groups", None))
    return jax.shard_map(
        functools.partial(on_device, mesh.shape["dp"]),
        mesh=mesh, in_specs=in_specs, out_specs=out_specs, check_vma=False,
    )
```

profile of v0, /device:TPU:0, one launch (start us, length us, event | category | flops | bytes accessed | tf_op | source)
XLA Modules:
  0.0 85.0 jit_solution(3173846341869231439)
XLA Ops:
  0.6 1.6 %copy.12.pm_ref = bf16[256,192]{1,0:T(8,128)(2,1)} copy(bf16[256,192]{0,1:T(8,128)(2,1)} %param.15) | data formatting | bytes 196608 | tf_op args[5]
  2.3 2.0 %copy.13.ph_ref = bf16[896,192]{1,0:T(8,128)(2,1)} copy(bf16[896,192]{0,1:T(8,128)(2,1)} %param.16) | data formatting | bytes 688128 | tf_op args[6]
  4.2 76.7 %sketch_scores.1 = (f32[16,3,64,64]{3,2,1,0:T(8,128)}, f32[16,32]{1,0:T(8,128)}) custom-call(bf16[2,4,4096]{2,1,0:T(4,128)(2,1)} %bitcast.7, bf16[2,4,4096]{2,1,0:T(4,128)(2,1)} %bitcast.8, bf16[896,8192]{1,0:T(8,128)(2,1)} %wg_ref.1, bf16[896,8192]{1,0:T(8,128)(2,1)} %wu_ref.1, bf16[896,8192]{1,0:T(8,128)(2,1)} %wd_ref.1, bf16[256,192]{1,0:T(8,128)(2,1)} %copy.12.pm_ref, ...), custom_call_target="tpu_custom_call" | custom-call | tf_op jit(solution)/shard_map/sketch_scores/pallas_call | solution.py:375
  81.0 2.7 %copy.16 = f32[16,3,64,64]{3,2,1,0:T(8,128)} copy(f32[16,3,64,64]{3,2,1,0:T(8,128)} %get-tuple-element.4) | data formatting | bytes 1572864
  83.7 1.3 %copy.17 = f32[16,32]{1,0:T(8,128)} copy(f32[16,32]{1,0:T(8,128)} %get-tuple-element.5) | data formatting | bytes 4096
where the time goes:
time: 85.3 us; the launch traced here: 85 us
  Pallas kernels  76.7 us (90%)
  local copies, waits for them, and re-layouts  7.62 us (9%)
    pallas_call x1, Pallas kernels, on_device(): pl.pallas_call(functools.partial(kernel, n), out_shape=(jax.ShapeDtypeStr...  76.7 us
    unnamed x4, local copies, waits for them, and re-layouts  7.62 us

commit v1 on v0

v1 whole, which is shorter than its diff:
```python
import functools

import jax
import jax.numpy as jnp
from jax import lax
from jax.experimental import pallas as pl
from jax.experimental.pallas import tpu as pltpu
from jax.sharding import PartitionSpec as P

DOMAINS = 32
SEQS = 16
MESH = pl.DeviceIdType.MESH
ROUTES = 2
CHUNKS = 8
TILE = 8


def routes_of(n):
    core = (2, 1)
    if n == 32:
        z, y, x = (4, 8), (2, 4), (2, 2)
        return ((z, y, x, core), (z, x, y, core))
    if n == 128:
        y, x = (8, 16), (8, 2)
        return ((y, x, core), (x, y, core))
    rest = (n // 2, 2)
    return ((rest, core), (rest, core))


def moved(index, size, stride, by):
    coord = lax.rem(lax.div(index, stride), size)
    return index + (lax.rem(coord + by, size) - coord) * stride


def kernel(
    n,
    act_ref, cot_ref, wg_ref, wu_ref, wd_ref, pm_ref, ph_ref, seq_ref, tgt_ref, dom_ref,
    sk_ref, score_ref,
    wbuf, xg, xs, gacc, uacc, dacc, pm, ph, tgt, tt, partl, partr, rsl, rsr, redl, redr, vl, vr, lm, msg, msgbuf,
    w_sem, own_sem, in_sem, ag_send, ag_recv, rs_send, rs_recv, bc_send, bc_recv, sc_send, sc_recv,
):
    me = lax.axis_index("dp")
    routes = routes_of(n)
    stages = len(routes[0])
    tokens, width = xs.shape[2], xs.shape[3]
    half_width = width // ROUTES
    rank = pm_ref.shape[0] // 3
    hidden_units = wg_ref.shape[0]
    own_rows = act_ref.shape[2]
    examples = tgt_ref.shape[0]
    tiles = partl.shape[0]

    def mult(r, stage):
        count = 1
        for size, _ in routes[r][:stage]:
            count = count * size
        return count

    def position(r, index, first=0):
        total = 0
        for i, (size, stride) in enumerate(routes[r]):
            if i >= first:
                if isinstance(index, int):
                    total += index // stride % size * mult(r, i)
                else:
                    total += lax.rem(lax.div(index, stride), size) * mult(r, i)
        return total

    def weight_copy(m, c):
        source = (wg_ref, wu_ref, wd_ref)[m]
        return pltpu.make_async_copy(
            source.at[:, pl.ds(c * width, width)], wbuf.at[m, c], w_sem.at[m, c]
        )

    own_copies = []
    for a, source in enumerate((act_ref, cot_ref)):
        for r in range(ROUTES):
            copy = pltpu.make_async_copy(
                source.at[:, r], xg.at[:, r, position(r, me), a], own_sem.at[a, r]
            )
            copy.start()
            own_copies.append(copy)

    barrier = pltpu.get_barrier_semaphore()
    partners = 0
    for size, stride in routes[0]:
        for d in range(1, size):
            pl.semaphore_signal(
                barrier, inc=1, device_id={"dp": moved(me, size, stride, d)}, device_id_type=MESH
            )
            partners += 1
    in_copies = [
        pltpu.make_async_copy(source, target, in_sem.at[i])
        for i, (source, target) in enumerate(((pm_ref, pm), (ph_ref, ph), (tgt_ref, tgt)))
    ]
    for m in range(3):
        weight_copy(m, 0).start()
    for copy in own_copies:
        copy.wait()
    pl.semaphore_wait(barrier, partners)

    def send_stage(c, r, stage):
        size, stride = routes[r][stage]
        blocks = xg.at[c, r, pl.ds(position(r, me, stage), mult(r, stage))]
        for d in range(1, size):
            pltpu.make_async_remote_copy(
                src_ref=blocks,
                dst_ref=blocks,
                send_sem=ag_send.at[r],
                recv_sem=ag_recv.at[c, r, stage],
                device_id={"dp": moved(me, size, stride, d)},
                device_id_type=MESH,
            ).start()

    def take_stage(c, r, stage):
        blocks = xg.at[c, r, pl.ds(0, mult(r, stage) * (routes[r][stage][0] - 1))]
        pltpu.make_async_copy(blocks, blocks, ag_recv.at[c, r, stage]).wait()

    def relay(c, stage):
        for r in range(ROUTES):
            take_stage(c, r, stage - 1)
            send_stage(c, r, stage)

    def first_sends(c, carry):
        for r in range(ROUTES):
            send_stage(c, r, 0)
        return carry

    def later_weights(c, carry):
        for m in range(3):
            weight_copy(m, c).start()
        return carry

    lax.fori_loop(0, CHUNKS, first_sends, 0)
    lax.fori_loop(1, CHUNKS, later_weights, 0)
    for copy in in_copies:
        copy.start()
    gacc[...] = jnp.zeros_like(gacc)
    uacc[...] = jnp.zeros_like(uacc)
    dacc[...] = jnp.zeros_like(dacc)

    def lay_out(a, c):
        group = 16 // own_rows
        for r in range(ROUTES):
            for g in range(tokens // 16):
                pieces = [
                    xg[c, r, position(r, g * group + i), a].astype(jnp.float32) for i in range(group)
                ]
                xs[a, c, g * 16 : (g + 1) * 16, r * half_width : (r + 1) * half_width] = jnp.concatenate(
                    pieces, 0
                ).astype(jnp.bfloat16)

    contract = (((1,), (1,)), ((), ()))

    def add_product(acc, a, m, c):
        weight_copy(m, c).wait()
        acc[...] += lax.dot_general(
            wbuf[m, c], xs[a, c], contract, preferred_element_type=jnp.float32
        )

    for lead in range(1, stages):
        for stage in range(1, lead + 1):
            relay(lead - stage, stage)

    def step(c, last=CHUNKS):
        relays = [(c + stages - stage, stage) for stage in range(stages - 1, 0, -1)]
        relays = [pair for i, pair in enumerate(relays) if i + 1 < last]
        for pair in relays[:1]:
            relay(*pair)
        for r in range(ROUTES):
            take_stage(c, r, stages - 1)
        lay_out(0, c)
        add_product(gacc, 0, 0, c)
        for pair in relays[1:2]:
            relay(*pair)
        add_product(uacc, 0, 1, c)
        for pair in relays[2:]:
            relay(*pair)
        lay_out(1, c)
        add_product(dacc, 1, 2, c)

    def looped(c, carry):
        step(c)
        return carry

    steady = CHUNKS - stages + 1
    lax.fori_loop(0, steady, looped, 0)
    for c in range(steady, CHUNKS):
        step(c, CHUNKS - c)

    for copy in in_copies:
        copy.wait()
    window = pm_ref.shape[1]
    model_cols = CHUNKS * width // n
    start = lax.div(me * model_cols, window) * window
    own_chunk = lax.div(start, width)
    own_cols = pl.ds(pl.multiple_of(lax.rem(start, width), window), window)

    def tiled(x):
        return x.reshape(x.shape[0] // TILE, TILE, tokens)

    split = 2 * rank // TILE
    partr[:split] = tiled(
        lax.dot_general(
            pm[: 2 * rank, :], xs[0, own_chunk, :, own_cols], contract, preferred_element_type=jnp.float32
        )
    )
    partr[split:] = tiled(
        lax.dot_general(
            pm[2 * rank :, :], xs[1, own_chunk, :, own_cols], contract, preferred_element_type=jnp.float32
        )
    )

    def owner_of(side, tile):
        owner = lax.div(tile * n, tiles)
        return n - 1 - owner if side else owner

    def side_of(side):
        index = n - 1 - me if side else me
        part, rsbuf, red, v = ((partl, rsl, redl, vl), (partr, rsr, redr, vr))[side]
        near = lax.div(index * tiles, n)
        mine = lax.div(index * tiles + n - 1, n)
        reduces = lax.div(mine * n, tiles) == index
        return part, rsbuf, red, v, near, mine, reduces

    def scatter(side):
        part, rsbuf, _, _, near, _, _ = side_of(side)

        def one(d, carry):
            tile = lax.rem(near + d, tiles)
            owner = owner_of(side, tile)

            @pl.when(owner == me)
            def _():
                pltpu.make_async_copy(part.at[tile], rsbuf.at[me], rs_recv.at[side]).start()

            @pl.when(owner != me)
            def _():
                pltpu.make_async_remote_copy(
                    src_ref=part.at[tile],
                    dst_ref=rsbuf.at[me],
                    send_sem=rs_send.at[side],
                    recv_sem=rs_recv.at[side],
                    device_id={"dp": owner},
                    device_id_type=MESH,
                ).start()

            return carry

        lax.fori_loop(0, tiles, one, 0)

    def share(side):
        part, rsbuf, red, v, _, mine, reduces = side_of(side)

        @pl.when(reduces)
        def _():
            pltpu.make_async_copy(rsbuf, rsbuf, rs_recv.at[side]).wait()
            red[...] = jnp.sum(rsbuf[...], 0)
            pltpu.make_async_copy(red, v.at[mine], bc_recv.at[side]).start()

            def one(d, carry):
                pltpu.make_async_remote_copy(
                    src_ref=red,
                    dst_ref=v.at[mine],
                    send_sem=bc_send.at[side],
                    recv_sem=bc_recv.at[side],
                    device_id={"dp": lax.rem(me + d, n)},
                    device_id_type=MESH,
                ).start()
                return carry

            lax.fori_loop(1, n, one, 0)

    def settle(side):
        part, rsbuf, red, v, _, _, reduces = side_of(side)

        @pl.when(reduces)
        def _():
            sent = part.at[pl.ds(0, tiles - 1)]
            pltpu.make_async_copy(sent, sent, rs_send.at[side]).wait()
            sent = rsbuf.at[pl.ds(0, n - 1)]
            pltpu.make_async_copy(sent, sent, bc_send.at[side]).wait()

        @pl.when(jnp.logical_not(reduces))
        def _():
            pltpu.make_async_copy(part, part, rs_send.at[side]).wait()

    scatter(1)
    in_down = out_gate = out_up = jnp.zeros((rank, tokens), jnp.float32)
    for off in range(0, hidden_units, 256):
        rows = slice(off, min(off + 256, hidden_units))
        gate, up, grad = gacc[rows], uacc[rows], dacc[rows]
        sig = jax.nn.sigmoid(gate)
        silu = gate * sig
        hidden = (silu * up).astype(jnp.bfloat16)
        grad_gate = (grad * up * sig * (1.0 + gate * (1.0 - sig))).astype(jnp.bfloat16)
        grad_up = (grad * silu).astype(jnp.bfloat16)
        in_down += jnp.dot(ph[:rank, rows], hidden, preferred_element_type=jnp.float32)
        out_gate += jnp.dot(ph[rank : 2 * rank, rows], grad_gate, preferred_element_type=jnp.float32)
        out_up += jnp.dot(ph[2 * rank :, rows], grad_up, preferred_element_type=jnp.float32)
    third = rank // TILE
    partl[:third] = tiled(out_gate)
    partl[third : 2 * third] = tiled(out_up)
    partl[2 * third :] = tiled(in_down)
    scatter(0)

    for e in range(examples):
        for k in range(3):
            piece = tgt[e, k].astype(jnp.float32)
            tt[k, e * rank : (e + 1) * rank, :] = jnp.concatenate([piece, piece], 1).astype(jnp.bfloat16)
    share(1)
    share(0)
    seq = seq_ref[...]
    lanes = lax.broadcasted_iota(jnp.int32, (1, examples * SEQS), 1)
    domains = jnp.zeros((1, examples * SEQS), jnp.int32)
    for e in range(examples):
        domains = jnp.where(lax.div(lanes, SEQS) == e, dom_ref[e], domains)
    msg[1:2] = domains.astype(jnp.float32)
    same = lax.broadcasted_iota(jnp.int32, (examples * SEQS, tokens), 0)
    same = jnp.where(lax.rem(same, SEQS) == seq, 1.0, 0.0).astype(jnp.bfloat16)

    pltpu.make_async_copy(vr, vr, bc_recv.at[1]).wait()
    rights = []
    products = []
    for k in range(3):
        right = vr[k * third : (k + 1) * third].reshape(rank, tokens)
        hi = right.astype(jnp.bfloat16)
        lo = (right - hi.astype(jnp.float32)).astype(jnp.bfloat16)
        rights.append((hi, lo))
        products.append(
            jnp.dot(tt[k], jnp.concatenate([hi, lo], 0), preferred_element_type=jnp.float32)
        )
    pltpu.make_async_copy(vl, vl, bc_recv.at[0]).wait()
    lefts = [vl[k * third : (k + 1) * third].reshape(rank, tokens) for k in range(3)]
    terms = jnp.zeros((examples, rank, tokens), jnp.float32)
    for k in range(3):
        terms += products[k].reshape(examples, rank, tokens) * lefts[k][None]
    term = jnp.sum(terms, 1)
    term_hi = term.astype(jnp.bfloat16).astype(jnp.float32)
    term_mid = (term - term_hi).astype(jnp.bfloat16).astype(jnp.float32)
    term_lo = term - term_hi - term_mid
    summed = lax.dot_general(
        jnp.concatenate([term_hi, term_mid, term_lo], 0).astype(jnp.bfloat16), same, contract,
        preferred_element_type=jnp.float32,
    )
    summed = summed[:examples] + summed[examples : 2 * examples] + summed[2 * examples :]
    row = lax.broadcasted_iota(jnp.int32, summed.shape, 0)
    lane = lax.broadcasted_iota(jnp.int32, summed.shape, 1)
    msg[0:1] = jnp.sum(jnp.where(lax.div(lane, SEQS) == row, summed, 0.0), 0, keepdims=True)
    pltpu.make_async_copy(msg, msgbuf.at[me], sc_recv).start()

    def spread(d, carry):
        pltpu.make_async_remote_copy(
            src_ref=msg,
            dst_ref=msgbuf.at[me],
            send_sem=sc_send,
            recv_sem=sc_recv,
            device_id={"dp": lax.rem(me + d, n)},
            device_id_type=MESH,
        ).start()
        return carry

    lax.fori_loop(1, n, spread, 0)

    squares = jnp.zeros((SEQS, TILE, rank), jnp.float32)
    for k in range(3):
        left_hi = lefts[k].astype(jnp.bfloat16).astype(jnp.float32)
        left_lo = lefts[k] - left_hi
        for s in range(SEQS):
            here = seq == s
            hi = jnp.where(here, left_hi, 0.0).astype(jnp.bfloat16)
            lo = jnp.where(here, left_lo, 0.0).astype(jnp.bfloat16)
            block = slice(s * rank, (s + 1) * rank)
            lm[block, :tokens] = hi
            lm[block, tokens : 2 * tokens] = lo
            lm[block, 2 * tokens :] = hi
        hi, lo = rights[k]
        sketch = lax.dot_general(
            lm[...], jnp.concatenate([hi, hi, lo], 1), contract, preferred_element_type=jnp.float32
        ).reshape(SEQS, rank, rank)
        sk_ref[:, k] = sketch
        for i in range(0, rank, TILE):
            piece = sketch[:, i : i + TILE]
            squares = squares + piece * piece
    inverse_norm = lax.rsqrt(jnp.sum(jnp.sum(squares, 1), 1, keepdims=True) + 1e-06)

    for side in range(2):
        settle(side)

    def sent_chunk(c, carry):
        for r in range(ROUTES):
            sent = xg.at[c, r, pl.ds(0, n - 1)]
            pltpu.make_async_copy(sent, sent, ag_send.at[r]).wait()
        return carry

    lax.fori_loop(0, CHUNKS, sent_chunk, 0)
    sent = msgbuf.at[pl.ds(0, n - 1)]
    pltpu.make_async_copy(sent, sent, sc_send).wait()
    pltpu.make_async_copy(msgbuf, msgbuf, sc_recv).wait()
    domain = lax.broadcasted_iota(jnp.int32, (DOMAINS, examples * SEQS), 0).astype(jnp.float32)
    total = jnp.zeros(domain.shape, jnp.float32)
    counts = jnp.zeros(domain.shape, jnp.float32)
    for i in range(n):
        got = msgbuf[i]
        here = got[1:2] == domain
        total += jnp.where(here, got[0:1], 0.0)
        counts += jnp.where(here, 1.0, 0.0)
    shift = SEQS
    while shift < examples * SEQS:
        total += pltpu.roll(total, shift, 1)
        counts += pltpu.roll(counts, shift, 1)
        shift *= 2
    score_ref[...] = (total / counts).T[:SEQS] * inverse_norm


def on_device(n, activations, cotangent, w_gate, w_up, w_down, proj_model, proj_hidden, seq_ids, targets, target_domain):
    own_rows, model = activations.shape
    tokens = n * own_rows
    hidden_units = w_gate.shape[0]
    model_cols, features = proj_model.shape
    rank = features // 3
    width = model // CHUNKS
    stages = len(routes_of(n)[0])
    examples = targets.shape[0]
    tiles = features // TILE

    def by_chunk(x):
        return x.reshape(own_rows, CHUNKS, ROUTES, width // ROUTES).transpose(1, 2, 0, 3)

    proj_model, proj_hidden = proj_model.T, proj_hidden.T
    if model_cols < 128:
        me = lax.axis_index("dp")
        padded = jnp.zeros((features, 128), proj_model.dtype)
        proj_model = lax.dynamic_update_slice(padded, proj_model, (0, (me * model_cols) % 128))
    vmem = pl.BlockSpec(memory_space=pltpu.VMEM)
    hbm = pl.BlockSpec(memory_space=pl.ANY)
    smem = pl.BlockSpec(memory_space=pltpu.SMEM)
    f32, bf16 = jnp.float32, jnp.bfloat16
    dma = pltpu.SemaphoreType.DMA
    return pl.pallas_call(
        functools.partial(kernel, n),
        out_shape=(
            jax.ShapeDtypeStruct((SEQS, 3, rank, rank), f32),
            jax.ShapeDtypeStruct((SEQS, DOMAINS), f32),
        ),
        in_specs=[hbm, hbm, hbm, hbm, hbm, hbm, hbm, vmem, hbm, smem],
        out_specs=(vmem, vmem),
        scratch_shapes=[
            pltpu.VMEM((3, CHUNKS, hidden_units, width), bf16),
            pltpu.VMEM((CHUNKS, ROUTES, n, 2, own_rows, width // ROUTES), bf16),
            pltpu.VMEM((2, CHUNKS, tokens, width), bf16),
            pltpu.VMEM((hidden_units, tokens), f32),
            pltpu.VMEM((hidden_units, tokens), f32),
            pltpu.VMEM((hidden_units, tokens), f32),
            pltpu.VMEM(proj_model.shape, bf16),
            pltpu.VMEM(proj_hidden.shape, bf16),
            pltpu.VMEM(targets.shape, bf16),
            pltpu.VMEM((3, examples * rank, 2 * rank), bf16),
            pltpu.VMEM((tiles, TILE, tokens), f32),
            pltpu.VMEM((tiles, TILE, tokens), f32),
            pltpu.VMEM((n, TILE, tokens), f32),
            pltpu.VMEM((n, TILE, tokens), f32),
            pltpu.VMEM((TILE, tokens), f32),
            pltpu.VMEM((TILE, tokens), f32),
            pltpu.VMEM((tiles, TILE, tokens), f32),
            pltpu.VMEM((tiles, TILE, tokens), f32),
            pltpu.VMEM((SEQS * rank, 3 * tokens), bf16),
            pltpu.VMEM((2, examples * SEQS), f32),
            pltpu.VMEM((n, 2, examples * SEQS), f32),
            dma((3, CHUNKS)),
            dma((2, ROUTES)),
            dma((3,)),
            dma((ROUTES,)),
            dma((CHUNKS, ROUTES, stages)),
            dma((2,)),
            dma((2,)),
            dma((2,)),
            dma((2,)),
            dma(()),
            dma(()),
        ],
        compiler_params=pltpu.CompilerParams(
            collective_id=0, has_side_effects=True, vmem_limit_bytes=67000000
        ),
        name="sketch_scores",
    )(
        by_chunk(activations), by_chunk(cotangent), w_gate, w_up, w_down, proj_model, proj_hidden,
        seq_ids.reshape(1, tokens), targets, target_domain,
    )


def solution(mesh):
    in_specs = (
        P(("groups", "dp"), None),
        P(("groups", "dp"), None),
        P("dp", None),
        P("dp", None),
        P("dp", None),
        P("dp", None),
        P("dp", None),
        P("groups"),
        P(("groups", "dp"), None, None, None),
        P(("groups", "dp")),
    )
    out_specs = (P("groups", None, None, None), P("groups", None))
    return jax.shard_map(
        functools.partial(on_device, mesh.shape["dp"]),
        mesh=mesh, in_specs=in_specs, out_specs=out_specs, check_vma=False,
    )
```

time: 85.3 us -> 75.1 us (0.88)
  Pallas kernels: 76.7 us -> 70.2 us
  local copies, waits for them, and re-layouts: 7.62 us -> 4.02 us
    pallas_call x1, Pallas kernels: 76.7 us -> 70.2 us  [on_device(): pl.pallas_call(functools.partial(kernel, n), out_shape=(jax.ShapeDtypeStr...]
    unnamed x4 -> x2, local copies, waits for them, and re-layouts: 7.62 us -> 4.02 us
where the time goes in v1:
time: 75.1 us; the launch traced here: 74.8 us
  Pallas kernels  70.2 us (93%)
  local copies, waits for them, and re-layouts  4.02 us (5%)
    pallas_call x1, Pallas kernels, on_device(): pl.pallas_call(functools.partial(kernel, n), out_shape=(jax.ShapeDtypeStr...  70.2 us
    unnamed x2, local copies, waits for them, and re-layouts  4.02 us

profile of v1, /device:TPU:0, one launch (start us, length us, event | category | flops | bytes accessed | tf_op | source)
XLA Modules:
  0.0 74.8 jit_solution(3356648182877374094)
XLA Ops:
  0.6 70.2 %sketch_scores.1 = (f32[16,3,64,64]{3,2,1,0:T(8,128)}, f32[16,32]{1,0:T(8,128)}) custom-call(bf16[8,2,4,512]{3,2,1,0:T(4,128)(2,1)} %bitcast.11, bf16[8,2,4,512]{3,2,1,0:T(4,128)(2,1)} %bitcast.12, bf16[896,8192]{1,0:T(8,128)(2,1)} %wg_ref.1, bf16[896,8192]{1,0:T(8,128)(2,1)} %wu_ref.1, bf16[896,8192]{1,0:T(8,128)(2,1)} %wd_ref.1, ...), custom_call_target="tpu_custom_call" | custom-call | tf_op jit(solution)/shard_map/sketch_scores/pallas_call | solution.py:440
  70.8 2.7 %copy.14 = f32[16,3,64,64]{3,2,1,0:T(8,128)} copy(f32[16,3,64,64]{3,2,1,0:T(8,128)} %get-tuple-element.4) | data formatting | bytes 1572864
  73.5 1.3 %copy.15 = f32[16,32]{1,0:T(8,128)} copy(f32[16,32]{1,0:T(8,128)} %get-tuple-element.5) | data formatting | bytes 4096

commit v2 on v1

--- a/solution.py
+++ b/solution.py
@@ -11,7 +11,11 @@
 SEQS = 16
 MESH = pl.DeviceIdType.MESH
 ROUTES = 2
-CHUNKS = 8
+CHUNKS = 16
+GROUP = 2
+EARLY = 0
+LAG = 3
+CORE_LAG = 2
 TILE = 8
 
 
@@ -19,12 +23,12 @@
     core = (2, 1)
     if n == 32:
         z, y, x = (4, 8), (2, 4), (2, 2)
-        return ((z, y, x, core), (z, x, y, core))
+        return ((z, y, x, core), (z, x, y, core), (y, z, x, core), (x, z, y, core))
     if n == 128:
         y, x = (8, 16), (8, 2)
-        return ((y, x, core), (x, y, core))
+        return ((y, x, core), (x, y, core)) * 2
     rest = (n // 2, 2)
-    return ((rest, core), (rest, core))
+    return ((rest, core),) * 4
 
 
 def moved(index, size, stride, by):
@@ -35,15 +39,16 @@
 def kernel(
     n,
     act_ref, cot_ref, wg_ref, wu_ref, wd_ref, pm_ref, ph_ref, seq_ref, tgt_ref, dom_ref,
-    sk_ref, score_ref,
-    wbuf, xg, xs, gacc, uacc, dacc, pm, ph, tgt, tt, partl, partr, rsl, rsr, redl, redr, vl, vr, lm, msg, msgbuf,
-    w_sem, own_sem, in_sem, ag_send, ag_recv, rs_send, rs_recv, bc_send, bc_recv, sc_send, sc_recv,
+    vl_ref, vr_ref, mean_ref,
+    wbuf, xg, xs, gacc, uacc, dacc, pm, ph, tgt, seqs, doms, tt, partl, partr, rsl, rsr, redl, redr, vl, vr, msg, msgbuf,
+    w_sem, own_sem, in_sem, out_sem, ag_send, ag_recv, rs_send, rs_recv, bc_send, bc_recv, sc_send, sc_recv,
 ):
     me = lax.axis_index("dp")
     routes = routes_of(n)
     stages = len(routes[0])
     tokens, width = xs.shape[2], xs.shape[3]
-    half_width = width // ROUTES
+    steps = xs.shape[1]
+    part_width = width // (GROUP * ROUTES)
     rank = pm_ref.shape[0] // 3
     hidden_units = wg_ref.shape[0]
     own_rows = act_ref.shape[2]
@@ -74,9 +79,13 @@
 
     own_copies = []
     for a, source in enumerate((act_ref, cot_ref)):
-        for r in range(ROUTES):
+        for route in range(2 * ROUTES):
+            r = route % ROUTES
+            chunks = pl.ds(0, EARLY) if route >= ROUTES else pl.ds(EARLY, CHUNKS - EARLY)
+            if chunks.size == 0:
+                continue
             copy = pltpu.make_async_copy(
-                source.at[:, r], xg.at[:, r, position(r, me), a], own_sem.at[a, r]
+                source.at[chunks, r], xg.at[chunks, r, position(route, me), a], own_sem.at[a, route]
             )
             copy.start()
             own_copies.append(copy)
@@ -91,7 +100,9 @@
             partners += 1
     in_copies = [
         pltpu.make_async_copy(source, target, in_sem.at[i])
-        for i, (source, target) in enumerate(((pm_ref, pm), (ph_ref, ph), (tgt_ref, tgt)))
+        for i, (source, target) in enumerate(
+            ((pm_ref, pm), (ph_ref, ph), (tgt_ref, tgt), (seq_ref, seqs), (dom_ref, doms))
+        )
     ]
     for m in range(3):
         weight_copy(m, 0).start()
@@ -99,9 +110,13 @@
         copy.wait()
     pl.semaphore_wait(barrier, partners)
 
+    def route_of(c, r):
+        return r + ROUTES if isinstance(c, int) and c < EARLY else r
+
     def send_stage(c, r, stage):
-        size, stride = routes[r][stage]
-        blocks = xg.at[c, r, pl.ds(position(r, me, stage), mult(r, stage))]
+        route = route_of(c, r)
+        size, stride = routes[route][stage]
+        blocks = xg.at[c, r, pl.ds(position(route, me, stage), mult(route, stage))]
         for d in range(1, size):
             pltpu.make_async_remote_copy(
                 src_ref=blocks,
@@ -113,7 +128,8 @@
             ).start()
 
     def take_stage(c, r, stage):
-        blocks = xg.at[c, r, pl.ds(0, mult(r, stage) * (routes[r][stage][0] - 1))]
+        route = route_of(c, r)
+        blocks = xg.at[c, r, pl.ds(0, mult(route, stage) * (routes[route][stage][0] - 1))]
         pltpu.make_async_copy(blocks, blocks, ag_recv.at[c, r, stage]).wait()
 
     def relay(c, stage):
@@ -131,8 +147,10 @@
             weight_copy(m, c).start()
         return carry
 
-    lax.fori_loop(0, CHUNKS, first_sends, 0)
-    lax.fori_loop(1, CHUNKS, later_weights, 0)
+    for c in range(EARLY):
+        first_sends(c, 0)
+    lax.fori_loop(EARLY, CHUNKS, first_sends, 0)
+    lax.fori_loop(1, steps, later_weights, 0)
     for copy in in_copies:
         copy.start()
     gacc[...] = jnp.zeros_like(gacc)
@@ -141,14 +159,16 @@
 
     def lay_out(a, c):
         group = 16 // own_rows
-        for r in range(ROUTES):
+        for part in range(GROUP * ROUTES):
+            h, r = part // ROUTES, part % ROUTES
             for g in range(tokens // 16):
                 pieces = [
-                    xg[c, r, position(r, g * group + i), a].astype(jnp.float32) for i in range(group)
+                    xg[c * GROUP + h, r, position(route_of(c * GROUP + h, r), g * group + i), a].astype(jnp.float32)
+                    for i in range(group)
                 ]
-                xs[a, c, g * 16 : (g + 1) * 16, r * half_width : (r + 1) * half_width] = jnp.concatenate(
-                    pieces, 0
-                ).astype(jnp.bfloat16)
+                xs[a, c, g * 16 : (g + 1) * 16, part * part_width : (part + 1) * part_width] = (
+                    jnp.concatenate(pieces, 0).astype(jnp.bfloat16)
+                )
 
     contract = (((1,), (1,)), ((), ()))
 
@@ -158,40 +178,39 @@
             wbuf[m, c], xs[a, c], contract, preferred_element_type=jnp.float32
         )
 
-    for lead in range(1, stages):
-        for stage in range(1, lead + 1):
-            relay(lead - stage, stage)
-
-    def step(c, last=CHUNKS):
-        relays = [(c + stages - stage, stage) for stage in range(stages - 1, 0, -1)]
-        relays = [pair for i, pair in enumerate(relays) if i + 1 < last]
-        for pair in relays[:1]:
-            relay(*pair)
-        for r in range(ROUTES):
-            take_stage(c, r, stages - 1)
+    def tick(i):
+        for stage in range(1, stages):
+            c = i - (stage - 1) * LAG
+            if not isinstance(c, int):
+                pl.when(c < CHUNKS)(functools.partial(relay, c, stage))
+            elif 0 <= c < CHUNKS:
+                relay(c, stage)
+
+    ahead = GROUP - 1 + (stages - 2) * LAG + CORE_LAG
+    for i in range(ahead):
+        tick(i)
+
+    def step(c, carry):
+        tick(c * GROUP + ahead)
+        for h in range(GROUP):
+            for r in range(ROUTES):
+                take_stage(c * GROUP + h, r, stages - 1)
         lay_out(0, c)
         add_product(gacc, 0, 0, c)
-        for pair in relays[1:2]:
-            relay(*pair)
+        tick(c * GROUP + ahead + 1)
         add_product(uacc, 0, 1, c)
-        for pair in relays[2:]:
-            relay(*pair)
         lay_out(1, c)
         add_product(dacc, 1, 2, c)
-
-    def looped(c, carry):
-        step(c)
         return carry
 
-    steady = CHUNKS - stages + 1
-    lax.fori_loop(0, steady, looped, 0)
-    for c in range(steady, CHUNKS):
-        step(c, CHUNKS - c)
+    for c in range(EARLY // GROUP):
+        step(c, 0)
+    lax.fori_loop(EARLY // GROUP, steps, step, 0)
 
     for copy in in_copies:
         copy.wait()
     window = pm_ref.shape[1]
-    model_cols = CHUNKS * width // n
+    model_cols = steps * width // n
     start = lax.div(me * model_cols, window) * window
     own_chunk = lax.div(start, width)
     own_cols = pl.ds(pl.multiple_of(lax.rem(start, width), window), window)
@@ -218,39 +237,39 @@
     def side_of(side):
         index = n - 1 - me if side else me
         part, rsbuf, red, v = ((partl, rsl, redl, vl), (partr, rsr, redr, vr))[side]
-        near = lax.div(index * tiles, n)
         mine = lax.div(index * tiles + n - 1, n)
         reduces = lax.div(mine * n, tiles) == index
-        return part, rsbuf, red, v, near, mine, reduces
+        return part, rsbuf, red, v, lax.rem(mine, tiles), reduces
 
     def scatter(side):
-        part, rsbuf, _, _, near, _, _ = side_of(side)
+        part, rsbuf, _, _, mine, reduces = side_of(side)
+
+        def send(tile):
+            pltpu.make_async_remote_copy(
+                src_ref=part.at[tile],
+                dst_ref=rsbuf.at[me],
+                send_sem=rs_send.at[side],
+                recv_sem=rs_recv.at[side],
+                device_id={"dp": owner_of(side, tile)},
+                device_id_type=MESH,
+            ).start()
 
         def one(d, carry):
-            tile = lax.rem(near + d, tiles)
-            owner = owner_of(side, tile)
-
-            @pl.when(owner == me)
-            def _():
-                pltpu.make_async_copy(part.at[tile], rsbuf.at[me], rs_recv.at[side]).start()
-
-            @pl.when(owner != me)
-            def _():
-                pltpu.make_async_remote_copy(
-                    src_ref=part.at[tile],
-                    dst_ref=rsbuf.at[me],
-                    send_sem=rs_send.at[side],
-                    recv_sem=rs_recv.at[side],
-                    device_id={"dp": owner},
-                    device_id_type=MESH,
-                ).start()
-
+            send(lax.rem(mine + d, tiles))
             return carry
 
-        lax.fori_loop(0, tiles, one, 0)
+        lax.fori_loop(1, tiles, one, 0, unroll=True)
+
+        @pl.when(reduces)
+        def _():
+            pltpu.make_async_copy(part.at[mine], rsbuf.at[me], rs_recv.at[side]).start()
+
+        @pl.when(jnp.logical_not(reduces))
+        def _():
+            send(mine)
 
     def share(side):
-        part, rsbuf, red, v, _, mine, reduces = side_of(side)
+        part, rsbuf, red, v, mine, reduces = side_of(side)
 
         @pl.when(reduces)
         def _():
@@ -269,10 +288,10 @@
                 ).start()
                 return carry
 
-            lax.fori_loop(1, n, one, 0)
+            lax.fori_loop(1, n, one, 0, unroll=n <= 32)
 
     def settle(side):
-        part, rsbuf, red, v, _, _, reduces = side_of(side)
+        part, rsbuf, red, v, _, reduces = side_of(side)
 
         @pl.when(reduces)
         def _():
@@ -310,27 +329,31 @@
             tt[k, e * rank : (e + 1) * rank, :] = jnp.concatenate([piece, piece], 1).astype(jnp.bfloat16)
     share(1)
     share(0)
-    seq = seq_ref[...]
+    seq = seqs[...]
     lanes = lax.broadcasted_iota(jnp.int32, (1, examples * SEQS), 1)
     domains = jnp.zeros((1, examples * SEQS), jnp.int32)
     for e in range(examples):
-        domains = jnp.where(lax.div(lanes, SEQS) == e, dom_ref[e], domains)
+        domains = jnp.where(lax.div(lanes, SEQS) == e, doms[e], domains)
     msg[1:2] = domains.astype(jnp.float32)
     same = lax.broadcasted_iota(jnp.int32, (examples * SEQS, tokens), 0)
     same = jnp.where(lax.rem(same, SEQS) == seq, 1.0, 0.0).astype(jnp.bfloat16)
 
     pltpu.make_async_copy(vr, vr, bc_recv.at[1]).wait()
-    rights = []
+    out_copies = [
+        pltpu.make_async_copy(v, out, out_sem.at[side])
+        for side, (v, out) in enumerate(((vl, vl_ref), (vr, vr_ref)))
+    ]
+    out_copies[1].start()
     products = []
     for k in range(3):
         right = vr[k * third : (k + 1) * third].reshape(rank, tokens)
         hi = right.astype(jnp.bfloat16)
         lo = (right - hi.astype(jnp.float32)).astype(jnp.bfloat16)
-        rights.append((hi, lo))
         products.append(
             jnp.dot(tt[k], jnp.concatenate([hi, lo], 0), preferred_element_type=jnp.float32)
         )
     pltpu.make_async_copy(vl, vl, bc_recv.at[0]).wait()
+    out_copies[0].start()
     lefts = [vl[k * third : (k + 1) * third].reshape(rank, tokens) for k in range(3)]
     terms = jnp.zeros((examples, rank, tokens), jnp.float32)
     for k in range(3):
@@ -360,29 +383,7 @@
         ).start()
         return carry
 
-    lax.fori_loop(1, n, spread, 0)
-
-    squares = jnp.zeros((SEQS, TILE, rank), jnp.float32)
-    for k in range(3):
-        left_hi = lefts[k].astype(jnp.bfloat16).astype(jnp.float32)
-        left_lo = lefts[k] - left_hi
-        for s in range(SEQS):
-            here = seq == s
-            hi = jnp.where(here, left_hi, 0.0).astype(jnp.bfloat16)
-            lo = jnp.where(here, left_lo, 0.0).astype(jnp.bfloat16)
-            block = slice(s * rank, (s + 1) * rank)
-            lm[block, :tokens] = hi
-            lm[block, tokens : 2 * tokens] = lo
-            lm[block, 2 * tokens :] = hi
-        hi, lo = rights[k]
-        sketch = lax.dot_general(
-            lm[...], jnp.concatenate([hi, hi, lo], 1), contract, preferred_element_type=jnp.float32
-        ).reshape(SEQS, rank, rank)
-        sk_ref[:, k] = sketch
-        for i in range(0, rank, TILE):
-            piece = sketch[:, i : i + TILE]
-            squares = squares + piece * piece
-    inverse_norm = lax.rsqrt(jnp.sum(jnp.sum(squares, 1), 1, keepdims=True) + 1e-06)
+    lax.fori_loop(1, n, spread, 0, unroll=n <= 32)
 
     for side in range(2):
         settle(side)
@@ -410,7 +411,48 @@
         total += pltpu.roll(total, shift, 1)
         counts += pltpu.roll(counts, shift, 1)
         shift *= 2
-    score_ref[...] = (total / counts).T[:SEQS] * inverse_norm
+    mean_ref[...] = total / counts
+    for copy in out_copies:
+        copy.wait()
+
+
+def finish(vl_ref, vr_ref, mean_ref, seq_ref, sk_ref, score_ref, lm, held, sem):
+    tokens = seq_ref.shape[1]
+    rank = sk_ref.shape[3]
+    third = rank // TILE
+    contract = (((1,), (1,)), ((), ()))
+    seq = seq_ref[...]
+    squares = jnp.zeros((SEQS, TILE, rank), jnp.float32)
+    copies = []
+    for k in range(3):
+        left = vl_ref[k * third : (k + 1) * third].reshape(rank, tokens)
+        right = vr_ref[k * third : (k + 1) * third].reshape(rank, tokens)
+        right_hi = right.astype(jnp.bfloat16)
+        right_lo = (right - right_hi.astype(jnp.float32)).astype(jnp.bfloat16)
+        left_hi = left.astype(jnp.bfloat16).astype(jnp.float32)
+        left_lo = left - left_hi
+        for s in range(SEQS):
+            here = seq == s
+            hi = jnp.where(here, left_hi, 0.0).astype(jnp.bfloat16)
+            lo = jnp.where(here, left_lo, 0.0).astype(jnp.bfloat16)
+            block = slice(s * rank, (s + 1) * rank)
+            lm[block, :tokens] = hi
+            lm[block, tokens : 2 * tokens] = lo
+            lm[block, 2 * tokens :] = hi
+        sketch = lax.dot_general(
+            lm[...], jnp.concatenate([right_hi, right_hi, right_lo], 1), contract,
+            preferred_element_type=jnp.float32,
+        ).reshape(SEQS, rank, rank)
+        held[k] = sketch
+        copies.append(pltpu.make_async_copy(held.at[k], sk_ref.at[:, k], sem.at[k]))
+        copies[k].start()
+        for i in range(0, rank, TILE):
+            piece = sketch[:, i : i + TILE]
+            squares = squares + piece * piece
+    inverse_norm = lax.rsqrt(jnp.sum(jnp.sum(squares, 1), 1, keepdims=True) + 1e-06)
+    score_ref[...] = mean_ref[...].T[:SEQS] * inverse_norm
+    for copy in copies:
+        copy.wait()
 
 
 def on_device(n, activations, cotangent, w_gate, w_up, w_down, proj_model, proj_hidden, seq_ids, targets, target_domain):
@@ -419,13 +461,15 @@
     hidden_units = w_gate.shape[0]
     model_cols, features = proj_model.shape
     rank = features // 3
-    width = model // CHUNKS
+    steps = CHUNKS // GROUP
+    width = model // steps
+    part_width = width // (GROUP * ROUTES)
     stages = len(routes_of(n)[0])
     examples = targets.shape[0]
     tiles = features // TILE
 
     def by_chunk(x):
-        return x.reshape(own_rows, CHUNKS, ROUTES, width // ROUTES).transpose(1, 2, 0, 3)
+        return x.reshape(own_rows, CHUNKS, ROUTES, part_width).transpose(1, 2, 0, 3)
 
     proj_model, proj_hidden = proj_model.T, proj_hidden.T
     if model_cols < 128:
@@ -434,27 +478,30 @@
         proj_model = lax.dynamic_update_slice(padded, proj_model, (0, (me * model_cols) % 128))
     vmem = pl.BlockSpec(memory_space=pltpu.VMEM)
     hbm = pl.BlockSpec(memory_space=pl.ANY)
-    smem = pl.BlockSpec(memory_space=pltpu.SMEM)
     f32, bf16 = jnp.float32, jnp.bfloat16
     dma = pltpu.SemaphoreType.DMA
-    return pl.pallas_call(
+    sequences = seq_ids.reshape(1, tokens)
+    lefts, rights, means = pl.pallas_call(
         functools.partial(kernel, n),
         out_shape=(
-            jax.ShapeDtypeStruct((SEQS, 3, rank, rank), f32),
-            jax.ShapeDtypeStruct((SEQS, DOMAINS), f32),
+            jax.ShapeDtypeStruct((tiles, TILE, tokens), f32),
+            jax.ShapeDtypeStruct((tiles, TILE, tokens), f32),
+            jax.ShapeDtypeStruct((DOMAINS, examples * SEQS), f32),
         ),
-        in_specs=[hbm, hbm, hbm, hbm, hbm, hbm, hbm, vmem, hbm, smem],
-        out_specs=(vmem, vmem),
+        in_specs=[hbm] * 10,
+        out_specs=(hbm, hbm, vmem),
         scratch_shapes=[
-            pltpu.VMEM((3, CHUNKS, hidden_units, width), bf16),
-            pltpu.VMEM((CHUNKS, ROUTES, n, 2, own_rows, width // ROUTES), bf16),
-            pltpu.VMEM((2, CHUNKS, tokens, width), bf16),
+            pltpu.VMEM((3, steps, hidden_units, width), bf16),
+            pltpu.VMEM((CHUNKS, ROUTES, n, 2, own_rows, part_width), bf16),
+            pltpu.VMEM((2, steps, tokens, width), bf16),
             pltpu.VMEM((hidden_units, tokens), f32),
             pltpu.VMEM((hidden_units, tokens), f32),
             pltpu.VMEM((hidden_units, tokens), f32),
             pltpu.VMEM(proj_model.shape, bf16),
             pltpu.VMEM(proj_hidden.shape, bf16),
             pltpu.VMEM(targets.shape, bf16),
+            pltpu.VMEM((1, tokens), jnp.int32),
+            pltpu.SMEM((examples,), jnp.int32),
             pltpu.VMEM((3, examples * rank, 2 * rank), bf16),
             pltpu.VMEM((tiles, TILE, tokens), f32),
             pltpu.VMEM((tiles, TILE, tokens), f32),
@@ -464,12 +511,12 @@
             pltpu.VMEM((TILE, tokens), f32),
             pltpu.VMEM((tiles, TILE, tokens), f32),
             pltpu.VMEM((tiles, TILE, tokens), f32),
-            pltpu.VMEM((SEQS * rank, 3 * tokens), bf16),
             pltpu.VMEM((2, examples * SEQS), f32),
             pltpu.VMEM((n, 2, examples * SEQS), f32),
-            dma((3, CHUNKS)),
-            dma((2, ROUTES)),
-            dma((3,)),
+            dma((3, steps)),
+            dma((2, 2 * ROUTES)),
+            dma((5,)),
+            dma((2,)),
             dma((ROUTES,)),
             dma((CHUNKS, ROUTES, stages)),
             dma((2,)),
@@ -485,8 +532,23 @@
         name="sketch_scores",
     )(
         by_chunk(activations), by_chunk(cotangent), w_gate, w_up, w_down, proj_model, proj_hidden,
-        seq_ids.reshape(1, tokens), targets, target_domain,
+        sequences, targets, target_domain,
     )
+    return pl.pallas_call(
+        finish,
+        out_shape=(
+            jax.ShapeDtypeStruct((SEQS, 3, rank, rank), f32),
+            jax.ShapeDtypeStruct((SEQS, DOMAINS), f32),
+        ),
+        in_specs=[vmem] * 4,
+        out_specs=(hbm, vmem),
+        scratch_shapes=[
+            pltpu.VMEM((SEQS * rank, 3 * tokens), bf16),
+            pltpu.VMEM((3, SEQS, rank, rank), f32),
+            dma((3,)),
+        ],
+        name="finish",
+    )(lefts, rights, means, sequences)
 
 
 def solution(mesh):

time: 75.1 us -> 60.6 us (0.81)
  Pallas kernels: 70.2 us -> 59.8 us
  local copies, waits for them, and re-layouts: 4.02 us -> 0 us
    pallas_call x1, Pallas kernels: 70.2 us -> 56.4 us  [on_device(): pl.pallas_call(functools.partial(kernel, n), out_shape=(jax.ShapeDtypeStr...]
    unnamed x2 -> x0, local copies, waits for them, and re-layouts: 4.02 us -> none
    pallas_call x0 -> x1, Pallas kernels: none -> 3.4 us  [on_device(): pl.pallas_call(finish, out_shape=(jax.ShapeDtypeStruct((SEQS, 3, rank, ra...]
where the time goes in v2:
time: 60.6 us; the launch traced here: 60.5 us
  Pallas kernels  59.8 us (99%)
  between operations  0.64 us (1%)
    pallas_call x1, Pallas kernels, on_device(): pl.pallas_call(functools.partial(kernel, n), out_shape=(jax.ShapeDtypeStr...  56.4 us
    pallas_call x1, Pallas kernels, on_device(): pl.pallas_call(finish, out_shape=(jax.ShapeDtypeStruct((SEQS, 3, rank, ra...  3.4 us

profile of v2, /device:TPU:0, one launch (start us, length us, event | category | flops | bytes accessed | tf_op | source)
XLA Modules:
  0.0 60.5 jit_solution(4158964400758644631)
XLA Ops:
  0.6 56.4 %sketch_scores.1 = (f32[24,8,128]{2,1,0:T(8,128)}, f32[24,8,128]{2,1,0:T(8,128)}, f32[32,128]{1,0:T(8,128)}) custom-call(bf16[16,2,4,256]{3,2,1,0:T(4,128)(2,1)} %bitcast.11, bf16[16,2,4,256]{3,2,1,0:T(4,128)(2,1)} %bitcast.12, bf16[896,8192]{1,0:T(8,128)(2,1)} %wg_ref.1, bf16[896,8192]{1,0:T(8,128)(2,1)} %wu_ref.1, bf16[896,8192]{1,0:T(8,128)(2,1)} %wd_ref.1, ...), custom_call_target="tpu_custom_call" | custom-call | tf_op jit(solution)/shard_map/sketch_scores/pallas_call | solution.py:484
  57.1 3.4 %finish.1 = (f32[16,3,64,64]{3,2,1,0:T(8,128)}, f32[16,32]{1,0:T(8,128)}) custom-call(f32[24,8,128]{2,1,0:T(8,128)} %get-tuple-element.5.vl_ref, f32[24,8,128]{2,1,0:T(8,128)} %get-tuple-element.6.vr_ref, f32[32,128]{1,0:T(8,128)} %get-tuple-element.7.mean_ref, s32[1,128]{1,0:T(1,128)} %bitcast.14), custom_call_target="tpu_custom_call" | custom-call | tf_op jit(solution)/shard_map/finish/pallas_call | solution.py:537
